TPU v7x, 32 devices: a whole 2x2x4 slice. The times are simulated.
32 devices in a mesh: groups: 2 (over y), hist: 4 (over z), head: 2 (over x), rep: 2 (over core).
Axes of the slice: x: 2, y: 2, z: 4, core: 2. Of those that a mesh axis runs over, the one named last changes fastest.
Arguments:
- item_feats: bfloat16 [4096, 4096], P(('groups', 'hist', 'rep')), parts along dimension 0, may hold values from -6 to 6
- adapter: bfloat16 [4096, 512], P('hist', 'head'), may hold values from -0.09375 to 0.09375
- hist_emb: bfloat16 [8192, 512], P(('groups', 'hist')), parts along dimension 0, may hold values from -6 to 6
- key_weight: bfloat16 [512, 512], P(None, 'head'), may hold values from -0.25 to 0.25
- value_weight: bfloat16 [512, 512], P(None, 'head'), may hold values from -0.25 to 0.25
- routes: int32 [4096, 1], P(('groups', 'hist', 'rep')), parts along dimension 0, may hold values from 0 to 3; in each aligned block of 256 rows (0 to 255, 256 to 511, ...) at most 128 rows name the same one
- cand_index: int32 [1024], P(('groups', 'hist', 'rep')), parts along dimension 0, may hold values from 0 to 255
- item_user: int32 [4096], P(('groups', 'hist', 'rep')), parts along dimension 0, may hold values from 0 to 255
- hist_user: int32 [8192], P(('groups', 'hist')), parts along dimension 0, may hold values from 0 to 255
Outputs:
- scored: bfloat16 [1024, 512], P(('groups', 'hist', 'rep'), 'head'), parts along dimension 0
There are 2 independent parts, one for each index of `groups`. A program takes and returns all parts, laid end to end along the dimension named above; an argument that names none is the same for every part. Nothing has to cross between parts.
Inputs may be any that keep to these rules, and one draw needn't show every extreme that they name: `routes`: in the rows of one device no owner is named more than 128 times; some owner is named exactly 128 times.
All inputs are finite; a program needn't handle non-finite values.
Results may differ from a plain program's by a relative error of at most 0.0081.
Values may be sent and summed in bfloat16 or wider, within the bound.
A program may use at most 64 MiB of HBM per device.

v0:
```python
import math
import jax
import jax.numpy as jnp
from jax import lax
from jax.sharding import PartitionSpec as P

HS = 64


def attend(query_block, user_block, key_rows, value_rows, key_users):
    row_count = query_block.shape[0]
    col_count = query_block.shape[1]
    heads_here = col_count // HS
    att_scale = float(HS) ** (-0.5)
    query_three = query_block.reshape(row_count, heads_here, HS)
    key_three = key_rows.reshape(-1, heads_here, HS)
    value_three = value_rows.reshape(-1, heads_here, HS)
    scores = (
        jnp.einsum("rhd,khd->hrk", query_three, key_three, preferred_element_type=jnp.float32)
        * att_scale
    )
    matching = user_block[:, None] == key_users[None, :]
    weights = jnp.where(matching[None], jax.nn.silu(scores), 0.0).astype(jnp.bfloat16)
    mixture = jnp.einsum("hrk,khd->rhd", weights, value_three, preferred_element_type=jnp.float32)
    counted = jnp.sum(matching.astype(jnp.float32), axis=1)
    inverse = 1.0 / jnp.maximum(counted, 1.0)
    return mixture.reshape(row_count, col_count) * inverse[:, None]


def dense_partial(queries, users, key_rows, value_rows, key_users):
    total_rows = queries.shape[0]
    col_count = queries.shape[1]
    block_size = math.gcd(total_rows, 512)
    blocked_queries = queries.reshape(total_rows // block_size, block_size, col_count)
    blocked_users = users.reshape(total_rows // block_size, block_size)

    def one_block(operands):
        return attend(operands[0], operands[1], key_rows, value_rows, key_users)

    return lax.map(one_block, (blocked_queries, blocked_users)).reshape(total_rows, col_count)


def body(
    item_feats,
    adapter,
    hist_emb,
    key_weight,
    value_weight,
    routes,
    cand_index,
    item_user,
    hist_user,
):
    owners = lax.axis_size("hist")
    item_count = item_feats.shape[0]
    col_count = adapter.shape[1]
    embedded = jnp.dot(
        item_feats,
        lax.all_gather(adapter, "hist", axis=0, tiled=True),
        preferred_element_type=jnp.float32,
    ).astype(jnp.bfloat16)
    capacity = 2 * item_count // owners
    owner_of = routes[:, 0]
    owner_hot = (owner_of[:, None] == jnp.arange(owners, dtype=jnp.int32)[None, :]).astype(
        jnp.int32
    )
    earlier = jnp.cumsum(owner_hot, axis=0) - owner_hot
    slot_of = jnp.sum(earlier * owner_hot, axis=1)
    position = owner_of * capacity + slot_of
    placing = (jnp.arange(owners * capacity, dtype=jnp.int32)[:, None] == position[None, :]).astype(
        jnp.bfloat16
    )
    outgoing = jnp.dot(placing, embedded, preferred_element_type=jnp.float32).astype(jnp.bfloat16)
    outgoing = outgoing.reshape(owners, capacity, col_count)
    shifted_user = (item_user + 1).astype(jnp.bfloat16)
    outgoing_user = (
        jnp.dot(placing, shifted_user, preferred_element_type=jnp.float32) - 1.0
    ).astype(jnp.bfloat16)
    outgoing_user = outgoing_user.reshape(owners, capacity)
    incoming, incoming_user = (
        lax.all_to_all(outgoing, "hist", split_axis=0, concat_axis=0, tiled=True),
        lax.all_to_all(outgoing_user, "hist", split_axis=0, concat_axis=0, tiled=True),
    )
    routed, routed_user = (
        lax.all_gather(incoming, "rep", axis=0, tiled=True),
        lax.all_gather(incoming_user, "rep", axis=0, tiled=True),
    )
    routed = routed.reshape(-1, col_count)
    routed_user = routed_user.reshape(-1)
    key_local = jnp.dot(hist_emb, key_weight, preferred_element_type=jnp.float32).astype(
        jnp.bfloat16
    )
    value_local = jnp.dot(hist_emb, value_weight, preferred_element_type=jnp.float32).astype(
        jnp.bfloat16
    )
    key_rows = jnp.concatenate([key_local, routed], axis=0)
    value_rows = jnp.concatenate([value_local, routed], axis=0)
    key_users = jnp.concatenate([hist_user.astype(jnp.bfloat16), routed_user], axis=0)
    own_queries = embedded[cand_index]
    own_users = item_user[cand_index].astype(jnp.bfloat16)
    gathered, gathered_users = (
        lax.all_gather(own_queries, "hist", axis=0, tiled=True),
        lax.all_gather(own_users, "hist", axis=0, tiled=True),
    )
    partial_value = dense_partial(gathered, gathered_users, key_rows, value_rows, key_users)
    attended = lax.psum_scatter(partial_value, "hist", scatter_dimension=0, tiled=True)
    gating = jax.nn.silu(own_queries.astype(jnp.float32))
    return (gating * attended).astype(jnp.bfloat16)


def solution(mesh):
    placed = (
        P(("groups", "hist", "rep"), None),
        P("hist", "head"),
        P(("groups", "hist"), None),
        P(None, "head"),
        P(None, "head"),
        P(("groups", "hist", "rep"), None),
        P(("groups", "hist", "rep")),
        P(("groups", "hist", "rep")),
        P(("groups", "hist")),
    )
    return jax.shard_map(
        body,
        mesh=mesh,
        in_specs=placed,
        out_specs=P(("groups", "hist", "rep"), "head"),
        check_vma=False,
    )
```

profile of v0, /device:TPU:0, one launch (start us, length us, event | category | flops | bytes accessed | tf_op | source)
XLA Modules:
  0.0 119.3 jit_solution(5111718014451120370)
XLA Ops:
  6.6 0.7 all-gather.4.cloned.1.call-update
  7.3 0.8 add_convert_fusion.1
  8.1 0.7 compare_convert_fusion
  8.7 1.2 %reduce-window.6 = s32[4,2,128]{2,1,0:T(2,128)S(1)} reduce-window(s32[4,2,128]{2,1,0:T(2,128)S(1)} %compare_convert_fusion, s32[]{:T(128)} %constant.17.clone.1), window={size=1x1x128 pad=0_0x0_0x127_0}, to_apply=%region_0.0 | reduce-window | flops 130048 | bytes 8196 | tf_op jit(solution)/shard_map/reduce-window
  10.3 0.7 fusion.14
  11.0 0.7 multiply_add_fusion
  11.9 0.6 copy.23
  12.5 6.3 %all-to-all-start.1 = ((bf16[4,1,128]{2,1,0:T(2,128)(2,1)}), bf16[4,1,128]{2,1,0:T(2,128)(2,1)S(1)}, u32[]{:S(2)}, u32[]{:S(2)}) async-start(bf16[4,1,128]{2,1,0:T(2,128)(2,1)} %copy.23), calls=%async_computation.1 | async-start | bytes 4096 | tf_op jit(solution)/shard_map/all_to_all | solution.py:82
  18.9 0.7 compare_select_fusion
  19.5 2.7 %convolution_convert_fusion = bf16[1024,256]{0,1:T(8,128)(2,1)} fusion(bf16[1024,512]{1,0:T(8,128)(2,1)} %param.11, bf16[512,256]{1,0:T(8,128)(2,1)} %param.12), kind=kOutput, calls=%fused_computation.5 | convolution fusion | flops 268697600 | bytes 1835008 | tf_op jit(solution)/shard_map/dot_general | solution.py:90
  22.2 1.3 %convolution_convert_fusion.1 = bf16[1024,256]{0,1:T(8,128)(2,1)} fusion(bf16[1024,512]{1,0:T(8,128)(2,1)S(1)} %copy-done.2, bf16[512,256]{1,0:T(8,128)(2,1)S(1)} %copy-done.5), kind=kOutput, calls=%fused_computation.6 | convolution fusion | flops 268697600 | bytes 1835008 | tf_op jit(solution)/shard_map/dot_general | solution.py:93
  23.6 0.8 gather_fusion.1
  24.4 0.6 dynamic-slice.2
  25.5 0.2 dynamic-update-slice
  25.7 12.6 %all-reduce = bf16[256]{0:T(256)(128)(2,1)S(1)} all-reduce(bf16[256]{0:T(256)(128)(2,1)S(1)} %dynamic-update-slice), channel_id=1, replica_groups=mesh['groups'=2,'hist'=4,'head'=2,'rep'=2] {'hist'}, use_global_device_ids=true, to_apply=%add | all-reduce | flops 256 | bytes 1024
  38.4 1.8 %all-gather = bf16[8,1,128]{2,1,0:T(2,128)(2,1)S(1)} all-gather(bf16[4,1,128]{2,1,0:T(2,128)(2,1)S(1)} %all-to-all-done.1), channel_id=2, replica_groups=mesh['groups'=2,'hist'=4,'head'=2,'rep'=2] {'rep'}, dimensions={0}, use_global_device_ids=true | all-gather | bytes 3072 | tf_op jit(solution)/shard_map/all_gather | solution.py:86
  40.2 0.4 convert_reduce_fusion
  40.6 17.1 %all-gather.4.cloned.1.call-done = bf16[4096,256]{1,0:T(8,128)(2,1)} async-done(((bf16[1024,256]{1,0:T(8,128)(2,1)}), bf16[4096,256]{1,0:T(8,128)(2,1)}) %all-gather.4.cloned.1.call-update) | async-done | bytes 2097168 | tf_op jit(solution)/shard_map/all_gather | solution.py:59
  57.7 2.3 %convolution_convert_fusion.3 = bf16[256,256]{1,0:T(8,128)(2,1)S(1)} fusion(bf16[256,4096]{1,0:T(8,128)(2,1)S(1)} %copy-done, bf16[4096,256]{1,0:T(8,128)(2,1)} %all-gather.4.cloned.1.call-done), kind=kOutput, calls=%fused_computation.10 | convolution fusion | flops 536936448 | bytes 4325376 | tf_op jit(solution)/shard_map/dot_general | solution.py:57
  60.0 0.9 convolution_convert_fusion.2
  60.9 3.4 %all-to-all-start = ((bf16[4,128,256]{2,1,0:T(8,128)(2,1)}), bf16[4,128,256]{2,1,0:T(8,128)(2,1)S(1)}, u32[]{:S(2)}, u32[]{:S(2)}) async-start(bf16[4,128,256]{2,1,0:T(8,128)(2,1)} %bitcast.5), calls=%async_computation | async-start | bytes 524288 | tf_op jit(solution)/shard_map/all_to_all | solution.py:81
  64.4 1.1 broadcast_compare_fusion
  65.5 0.7 gather_fusion
  66.2 14.3 %all-gather.1 = bf16[256,256]{1,0:T(8,128)(2,1)S(1)} all-gather(bf16[64,256]{1,0:T(8,128)(2,1)S(1)} %gather_fusion), channel_id=3, replica_groups=mesh['groups'=2,'hist'=4,'head'=2,'rep'=2] {'hist'}, dimensions={0}, use_global_device_ids=true | all-gather | bytes 163840 | tf_op jit(solution)/shard_map/all_gather | solution.py:102
  80.5 0.8 copy.24
  81.3 2.2 %all_gather.16 = bf16[8,128,256]{2,1,0:T(8,128)(2,1)S(1)} all-gather(bf16[4,128,256]{2,1,0:T(8,128)(2,1)S(1)} %all-to-all-done), channel_id=1, replica_groups=mesh['groups'=2,'hist'=4,'head'=2,'rep'=2] {'rep'}, dimensions={0}, use_global_device_ids=true | all-gather | bytes 786432 | tf_op jit(solution)/shard_map/all_gather | solution.py:85
  83.5 0.3 copy.22
  83.8 0.2 concatenate.18
  84.0 5.2 %fusion = f32[4,64,256]{2,1,0:T(8,128)S(1)} fusion(bf16[256,4,64]{0,2,1:T(8,128)(2,1)} %bitcast.47, pred[256,2048]{1,0:T(8,128)(4,1)} %broadcast_compare_fusion, bf16[1024,4,64]{0,2,1:T(8,128)(2,1)S(1)} %concatenate.18, bf16[1024,4,64]{0,2,1:T(8,128)(2,1)} %bitcast.45, bf16[1024,4,64]{0,2,1:T(8,128)(2,1)} %bitcast.44), kind=kOutput, calls=%fused_computation.4 | convolution fusion | flops 555745280 | bytes 2490368 | tf_op jit(solution)/shard_map/while/body/eval_jaxpr/hrk,khd->rhd/dot_general | solution.py:24
  89.4 0.8 broadcast_multiply_fusion
  90.2 20.8 %reduce-scatter.2.cloned.1.call-done = f32[64,256]{1,0:T(8,128)} async-done(((f32[256,256]{1,0:T(8,128)}), f32[64,256]{1,0:T(8,128)}) %reduce-scatter.2.cloned.1.call-update) | async-done | bytes 65552 | tf_op jit(solution)/shard_map/reduce_scatter | solution.py:106
  111.0 1.5 %fusion.11 = bf16[64,256]{1,0:T(8,128)(2,1)} fusion(f32[64,256]{1,0:T(8,128)} %reduce-scatter.2.cloned.1.call-done, bf16[64,256]{1,0:T(8,128)(2,1)S(1)} %copy-done.4), kind=kLoop, calls=%fused_computation.25 | loop fusion | flops 114688 | bytes 131072 | tf_op jit(solution)/shard_map/convert_element_type | solution.py:108
  (38 shorter events, 0.9 us)
Async XLA Ops:
  6.5 51.1 %copy-start = (bf16[256,4096]{1,0:T(8,128)(2,1)S(1)}, bf16[256,4096]{1,0:T(8,128)(2,1)}, u32[]{:S(2)}) copy-start(bf16[256,4096]{1,0:T(8,128)(2,1)} %param.9) | copy-start | bytes 6291460
  6.5 17.0 %copy-start.1 = (s32[256]{0:T(256)S(1)}, s32[256]{0:T(256)}, u32[]{:S(2)}) copy-start(s32[256]{0:T(256)} %param.16) | copy-start | bytes 3076
  6.5 15.7 %copy-start.2 = (bf16[1024,512]{1,0:T(8,128)(2,1)S(1)}, bf16[1024,512]{1,0:T(8,128)(2,1)}, u32[]{:S(2)}) copy-start(bf16[1024,512]{1,0:T(8,128)(2,1)} %param.11) | copy-start | bytes 3145732
  6.5 15.7 %copy-start.5 = (bf16[512,256]{1,0:T(8,128)(2,1)S(1)}, bf16[512,256]{1,0:T(8,128)(2,1)}, u32[]{:S(2)}) copy-start(bf16[512,256]{1,0:T(8,128)(2,1)} %param.13) | copy-start | bytes 786436
  6.5 17.0 %copy-start.6 = (s32[1024]{0:T(1024)S(1)}, s32[1024]{0:T(1024)}, u32[]{:S(2)}) copy-start(s32[1024]{0:T(1024)} %param.17) | copy-start | bytes 12292
  6.5 51.1 %all-gather.4.cloned.1.call-start = ((), (), s32[]{:S(2)}) async-start(), calls=%async_computation.3 | async-start | bytes 2621440 | tf_op jit(solution)/shard_map/all_gather | solution.py:59
  12.5 25.8 %all-to-all-start.1 = ((bf16[4,1,128]{2,1,0:T(2,128)(2,1)}), bf16[4,1,128]{2,1,0:T(2,128)(2,1)S(1)}, u32[]{:S(2)}, u32[]{:S(2)}) async-start(bf16[4,1,128]{2,1,0:T(2,128)(2,1)} %copy.23), calls=%async_computation.1 | async-start | bytes 4096 | tf_op jit(solution)/shard_map/all_to_all | solution.py:82
  19.5 4.8 %copy-start.7 = (u32[32]{0:T(128)S(1)}, u32[32]{0:T(128)}, u32[]{:S(2)}) copy-start(u32[32]{0:T(128)} %constant.42) | copy-start | bytes 388
  60.9 20.4 %all-to-all-start = ((bf16[4,128,256]{2,1,0:T(8,128)(2,1)}), bf16[4,128,256]{2,1,0:T(8,128)(2,1)S(1)}, u32[]{:S(2)}, u32[]{:S(2)}) async-start(bf16[4,128,256]{2,1,0:T(8,128)(2,1)} %bitcast.5), calls=%async_computation | async-start | bytes 524288 | tf_op jit(solution)/shard_map/all_to_all | solution.py:81
  64.3 46.7 %reduce-scatter.2.cloned.1.call-start = ((), (), s32[]{:S(2)}) async-start(), calls=%async_computation.4 | async-start | bytes 327680 | tf_op jit(solution)/shard_map/reduce_scatter | solution.py:106
  66.2 15.1 %copy-start.3 = (bf16[64,256]{1,0:T(8,128)(2,1)}, bf16[64,256]{1,0:T(8,128)(2,1)S(1)}, u32[]{:S(2)}) copy-start(bf16[64,256]{1,0:T(8,128)(2,1)S(1)} %gather_fusion) | copy-start | bytes 98308
  84.0 27.0 %copy-start.4 = (bf16[64,256]{1,0:T(8,128)(2,1)S(1)}, bf16[64,256]{1,0:T(8,128)(2,1)}, u32[]{:S(2)}) copy-start(bf16[64,256]{1,0:T(8,128)(2,1)} %copy-done.3) | copy-start | bytes 98308
Sparse Core Ops, SparseCore 0:
  8.9 48.7 all-gather.3
  90.3 20.6 reduce-scatter.1
where the time goes:
time: 120 us; the launch traced here: 119 us
  waiting for transfers between devices  38.6 us (32%)
  blocking collectives  30.9 us (26%)
  between operations  14.1 us (12%)
  matrix products  12.7 us (11%)
  starting transfers between devices  9.83 us (8%)
  other arithmetic  8.64 us (7%)
  local copies, waits for them, and re-layouts  4.62 us (4%)
    reduce_scatter x1, waiting for transfers between devices, body(): lax.psum_scatter(partial_value, 'hist', scatter_dimension=0, tiled=True)  20.8 us
    all_gather x1, waiting for transfers between devices, body(): lax.all_gather(adapter, 'hist', axis=0, tiled=True)  17.1 us
    all_gather x1, blocking collectives, body(): lax.all_gather(own_queries, 'hist', axis=0, tiled=True)  14.3 us
    unnamed x1, blocking collectives  12.6 us
    all_to_all x1, starting transfers between devices, body(): lax.all_to_all(outgoing_user, 'hist', split_axis=0, concat_axis=0, tiled=...  6.35 us
    dot_general x1, matrix products, attend(): jnp.einsum('hrk,khd->rhd', weights, value_three, preferred_element_type=j...  5.22 us
    all_to_all x1, starting transfers between devices, body(): lax.all_to_all(outgoing, 'hist', split_axis=0, concat_axis=0, tiled=True)  3.4 us
    dot_general x1, matrix products, body(): jnp.dot(hist_emb, key_weight, preferred_element_type=jnp.float32)  2.69 us
  transfers between devices with their start and end apart: 4, of which 2 were waited for; matrix products, arithmetic and copies ran while one was open for 12% of the time, Pallas kernels for 0%

commit v1 on v0

--- a/solution.py
+++ b/solution.py
@@ -54,11 +54,15 @@
     owners = lax.axis_size("hist")
     item_count = item_feats.shape[0]
     col_count = adapter.shape[1]
-    embedded = jnp.dot(
-        item_feats,
-        lax.all_gather(adapter, "hist", axis=0, tiled=True),
-        preferred_element_type=jnp.float32,
-    ).astype(jnp.bfloat16)
+
+    def find_cycles(array_here):
+        u_next = jnp.stack([array_here for _ in range(lax.axis_size("hist"))])
+        parts_out = lax.all_to_all(u_next, axis_name="hist", split_axis=0, concat_axis=0)
+        return jnp.concatenate(parts_out, axis=0)
+
+    embedded = jnp.dot(item_feats, find_cycles(adapter), preferred_element_type=jnp.float32).astype(
+        jnp.bfloat16
+    )
     capacity = 2 * item_count // owners
     owner_of = routes[:, 0]
     owner_hot = (owner_of[:, None] == jnp.arange(owners, dtype=jnp.int32)[None, :]).astype(

time: 120 us -> 147 us (1.23)
  blocking collectives: 30.9 us -> 66.8 us
  waiting for transfers between devices: 38.6 us -> 23.3 us
  starting transfers between devices: 9.83 us -> 15.2 us
  local copies, waits for them, and re-layouts: 4.62 us -> 6.55 us
    unnamed x1, blocking collectives: 12.6 us -> 36.5 us
    all_gather x1 -> x0, waiting for transfers between devices: 17.1 us -> none  [body(): lax.all_gather(adapter, 'hist', axis=0, tiled=True)]
    all_to_all x0 -> x1, blocking collectives: none -> 11.7 us  [body(): lax.all_to_all(outgoing_user, 'hist', split_axis=0, concat_axis=0, tiled=...]
    all_to_all x1, starting transfers between devices: 3.4 us -> 10.6 us  [body(): lax.all_to_all(outgoing, 'hist', split_axis=0, concat_axis=0, tiled=True)]
    all_to_all x1, waiting for transfers between devices: 0.01 us -> 2.66 us  [find_cycles(): lax.all_to_all(u_next, axis_name='hist', split_axis=0, concat_axis=0)]
    another operation x2 -> x3, local copies, waits for them, and re-layouts: 0.1 us -> 2.57 us  [the longest x1 2.47 us: find_cycles(): u_next = jnp.stack([array_here for _ in range(lax.axis_size('hist'))])]
    all_to_all x1, starting transfers between devices: 6.35 us -> 4.58 us  [find_cycles(): lax.all_to_all(u_next, axis_name='hist', split_axis=0, concat_axis=0)]
  transfers between devices with their start and end apart: 4 -> 3, of which waited for: 2 -> 2; matrix products, arithmetic and copies ran while one was open for 12% -> 6% of each run, Pallas kernels for 0% -> 0%
where the time goes in v1:
time: 147 us; the launch traced here: 146 us
  blocking collectives  66.8 us (45%)
  waiting for transfers between devices  23.3 us (16%)
  starting transfers between devices  15.2 us (10%)
  between operations  14.2 us (10%)
  matrix products  12.2 us (8%)
  other arithmetic  8.05 us (5%)
  local copies, waits for them, and re-layouts  6.55 us (4%)
    unnamed x1, blocking collectives  36.5 us
    reduce_scatter x1, waiting for transfers between devices, body(): lax.psum_scatter(partial_value, 'hist', scatter_dimension=0, tiled=True)  20.6 us
    all_gather x1, blocking collectives, body(): lax.all_gather(own_queries, 'hist', axis=0, tiled=True)  14.5 us
    all_to_all x1, blocking collectives, body(): lax.all_to_all(outgoing_user, 'hist', split_axis=0, concat_axis=0, tiled=...  11.7 us
    all_to_all x1, starting transfers between devices, body(): lax.all_to_all(outgoing, 'hist', split_axis=0, concat_axis=0, tiled=True)  10.6 us
    dot_general x1, matrix products, attend(): jnp.einsum('hrk,khd->rhd', weights, value_three, preferred_element_type=j...  5.23 us
    all_to_all x1, starting transfers between devices, find_cycles(): lax.all_to_all(u_next, axis_name='hist', split_axis=0, concat_axis=0)  4.58 us
  transfers between devices with their start and end apart: 3, of which 2 were waited for; matrix products, arithmetic and copies ran while one was open for 6% of the time, Pallas kernels for 0%

profile of v1, /device:TPU:0, one launch (start us, length us, event | category | flops | bytes accessed | tf_op | source)
XLA Modules:
  0.0 146.4 jit_solution(7994627517315313999)
XLA Ops:
  6.5 0.8 add_convert_fusion.1
  7.4 0.7 compare_convert_fusion
  8.1 1.2 reduce-window.6
  9.7 0.7 fusion.14
  10.4 0.7 multiply_add_fusion
  11.0 0.2 fusion.4
  11.3 11.7 %all_to_all.22 = bf16[4,1,128]{2,1,0:T(2,128)(2,1)S(1)} all-to-all(bf16[4,1,128]{2,1,0:T(2,128)(2,1)S(1)} %copy.23), channel_id=1, replica_groups=mesh['groups'=2,'hist'=4,'head'=2,'rep'=2] {'hist'}, dimensions={0} | all-to-all | bytes 2048 | tf_op jit(solution)/shard_map/all_to_all | solution.py:86
  23.0 2.5 %stack.2 = bf16[4,1024,256]{2,1,0:T(8,128)(2,1)} broadcast(bf16[1024,256]{1,0:T(8,128)(2,1)} %param.10), dimensions={1,2} | broadcast | bytes 2621440 | tf_op jit(solution)/shard_map/stack | solution.py:59
  25.5 4.6 %all-to-all-start = ((bf16[4,1024,256]{2,1,0:T(8,128)(2,1)}), bf16[4,1024,256]{2,1,0:T(8,128)(2,1)}, u32[]{:S(2)}, u32[]{:S(2)}) async-start(bf16[4,1024,256]{2,1,0:T(8,128)(2,1)} %stack.2), calls=%async_computation | async-start | bytes 4194304 | tf_op jit(solution)/shard_map/all_to_all | solution.py:60
  30.2 0.8 gather_fusion.1
  31.0 0.6 dynamic-slice.2
  32.2 0.2 dynamic-update-slice
  32.5 36.5 %all-reduce = bf16[256]{0:T(256)(128)(2,1)S(1)} all-reduce(bf16[256]{0:T(256)(128)(2,1)S(1)} %dynamic-update-slice), channel_id=1, replica_groups=mesh['groups'=2,'hist'=4,'head'=2,'rep'=2] {'hist'}, use_global_device_ids=true, to_apply=%add | all-reduce | flops 256 | bytes 1024
  69.0 1.3 convolution_convert_fusion.1
  70.3 2.3 %convolution_convert_fusion = bf16[1024,256]{0,1:T(8,128)(2,1)} fusion(bf16[1024,512]{1,0:T(8,128)(2,1)S(1)} %copy-done.2, bf16[512,256]{1,0:T(8,128)(2,1)} %param.12), kind=kOutput, calls=%fused_computation.5 | convolution fusion | flops 268697600 | bytes 1835008 | tf_op jit(solution)/shard_map/dot_general | solution.py:94
  72.5 1.8 %all-gather = bf16[8,1,128]{2,1,0:T(2,128)(2,1)S(1)} all-gather(bf16[4,1,128]{2,1,0:T(2,128)(2,1)S(1)} %all_to_all.22), channel_id=2, replica_groups=mesh['groups'=2,'hist'=4,'head'=2,'rep'=2] {'rep'}, dimensions={0}, use_global_device_ids=true | all-gather | bytes 3072 | tf_op jit(solution)/shard_map/all_gather | solution.py:90
  74.4 0.4 convert_reduce_fusion
  74.7 2.7 %all-to-all-done = bf16[4,1024,256]{2,1,0:T(8,128)(2,1)} async-done(((bf16[4,1024,256]{2,1,0:T(8,128)(2,1)}), bf16[4,1024,256]{2,1,0:T(8,128)(2,1)}, u32[]{:S(2)}, u32[]{:S(2)}) %all-to-all-start) | async-done | bytes 2097184 | tf_op jit(solution)/shard_map/all_to_all | solution.py:60
  77.4 2.3 %convolution_convert_fusion.3 = bf16[256,256]{1,0:T(8,128)(2,1)S(1)} fusion(bf16[256,4096]{1,0:T(8,128)(2,1)S(1)} %copy-done, bf16[4096,256]{1,0:T(8,128)(2,1)} %bitcast), kind=kOutput, calls=%fused_computation.10 | convolution fusion | flops 536936448 | bytes 4325376 | tf_op jit(solution)/shard_map/dot_general | solution.py:63
  79.7 0.9 convolution_convert_fusion.2
  80.7 10.6 %all-to-all-start.1 = ((bf16[4,128,256]{2,1,0:T(8,128)(2,1)}), bf16[4,128,256]{2,1,0:T(8,128)(2,1)S(1)}, u32[]{:S(2)}, u32[]{:S(2)}) async-start(bf16[4,128,256]{2,1,0:T(8,128)(2,1)} %bitcast.6), calls=%async_computation.1 | async-start | bytes 524288 | tf_op jit(solution)/shard_map/all_to_all | solution.py:85
  91.3 1.1 broadcast_compare_fusion
  92.4 0.7 gather_fusion
  93.1 14.5 %all-gather.1 = bf16[256,256]{1,0:T(8,128)(2,1)S(1)} all-gather(bf16[64,256]{1,0:T(8,128)(2,1)S(1)} %gather_fusion), channel_id=3, replica_groups=mesh['groups'=2,'hist'=4,'head'=2,'rep'=2] {'hist'}, dimensions={0}, use_global_device_ids=true | all-gather | bytes 163840 | tf_op jit(solution)/shard_map/all_gather | solution.py:106
  107.7 0.8 copy.24
  108.4 2.2 %all_gather.12 = bf16[8,128,256]{2,1,0:T(8,128)(2,1)S(1)} all-gather(bf16[4,128,256]{2,1,0:T(8,128)(2,1)S(1)} %all-to-all-done.1), channel_id=1, replica_groups=mesh['groups'=2,'hist'=4,'head'=2,'rep'=2] {'rep'}, dimensions={0}, use_global_device_ids=true | all-gather | bytes 786432 | tf_op jit(solution)/shard_map/all_gather | solution.py:89
  110.6 0.3 copy.22
  110.9 0.2 concatenate.18
  111.2 5.2 %fusion = f32[4,64,256]{2,1,0:T(8,128)S(1)} fusion(bf16[256,4,64]{0,2,1:T(8,128)(2,1)} %bitcast.48, pred[256,2048]{1,0:T(8,128)(4,1)} %broadcast_compare_fusion, bf16[1024,4,64]{0,2,1:T(8,128)(2,1)S(1)} %concatenate.18, bf16[1024,4,64]{0,2,1:T(8,128)(2,1)} %bitcast.45, bf16[1024,4,64]{0,2,1:T(8,128)(2,1)} %bitcast.46), kind=kOutput, calls=%fused_computation.4 | convolution fusion | flops 555745280 | bytes 2490368 | tf_op jit(solution)/shard_map/while/body/eval_jaxpr/hrk,khd->rhd/dot_general | solution.py:24
  116.6 0.8 broadcast_multiply_fusion
  117.4 20.6 %reduce-scatter.2.cloned.1.call-done = f32[64,256]{1,0:T(8,128)} async-done(((f32[256,256]{1,0:T(8,128)}), f32[64,256]{1,0:T(8,128)}) %reduce-scatter.2.cloned.1.call-update) | async-done | bytes 65552 | tf_op jit(solution)/shard_map/reduce_scatter | solution.py:110
  138.0 1.5 %fusion.11 = bf16[64,256]{1,0:T(8,128)(2,1)} fusion(f32[64,256]{1,0:T(8,128)} %reduce-scatter.2.cloned.1.call-done, bf16[64,256]{1,0:T(8,128)(2,1)S(1)} %copy-done.4), kind=kLoop, calls=%fused_computation.25 | loop fusion | flops 114688 | bytes 131072 | tf_op jit(solution)/shard_map/convert_element_type | solution.py:112
  (39 shorter events, 0.7 us)
Async XLA Ops:
  6.5 70.9 %copy-start = (bf16[256,4096]{1,0:T(8,128)(2,1)S(1)}, bf16[256,4096]{1,0:T(8,128)(2,1)}, u32[]{:S(2)}) copy-start(bf16[256,4096]{1,0:T(8,128)(2,1)} %param.9) | copy-start | bytes 6291460
  25.5 4.6 %copy-start.6 = (s32[1024]{0:T(1024)S(1)}, s32[1024]{0:T(1024)}, u32[]{:S(2)}) copy-start(s32[1024]{0:T(1024)} %param.17) | copy-start | bytes 12292
  25.5 4.7 %copy-start.7 = (s32[64]{0:T(128)S(1)}, s32[64]{0:T(128)}, u32[]{:S(2)}) copy-start(s32[64]{0:T(128)} %param.15) | copy-start | bytes 772
  25.5 4.7 %copy-start.1 = (s32[256]{0:T(256)S(1)}, s32[256]{0:T(256)}, u32[]{:S(2)}) copy-start(s32[256]{0:T(256)} %param.16) | copy-start | bytes 3076
  25.5 5.5 %copy-start.8 = (u32[32]{0:T(128)S(1)}, u32[32]{0:T(128)}, u32[]{:S(2)}) copy-start(u32[32]{0:T(128)} %constant.42) | copy-start | bytes 388
  25.5 43.5 %copy-start.2 = (bf16[1024,512]{1,0:T(8,128)(2,1)S(1)}, bf16[1024,512]{1,0:T(8,128)(2,1)}, u32[]{:S(2)}) copy-start(bf16[1024,512]{1,0:T(8,128)(2,1)} %param.11) | copy-start | bytes 3145732
  25.5 43.5 %copy-start.5 = (bf16[512,256]{1,0:T(8,128)(2,1)S(1)}, bf16[512,256]{1,0:T(8,128)(2,1)}, u32[]{:S(2)}) copy-start(bf16[512,256]{1,0:T(8,128)(2,1)} %param.13) | copy-start | bytes 786436
  25.5 51.9 %all-to-all-start = ((bf16[4,1024,256]{2,1,0:T(8,128)(2,1)}), bf16[4,1024,256]{2,1,0:T(8,128)(2,1)}, u32[]{:S(2)}, u32[]{:S(2)}) async-start(bf16[4,1024,256]{2,1,0:T(8,128)(2,1)} %stack.2), calls=%async_computation | async-start | bytes 4194304 | tf_op jit(solution)/shard_map/all_to_all | solution.py:60
  80.7 27.8 %all-to-all-start.1 = ((bf16[4,128,256]{2,1,0:T(8,128)(2,1)}), bf16[4,128,256]{2,1,0:T(8,128)(2,1)S(1)}, u32[]{:S(2)}, u32[]{:S(2)}) async-start(bf16[4,128,256]{2,1,0:T(8,128)(2,1)} %bitcast.6), calls=%async_computation.1 | async-start | bytes 524288 | tf_op jit(solution)/shard_map/all_to_all | solution.py:85
  91.3 46.7 %reduce-scatter.2.cloned.1.call-start = ((), (), s32[]{:S(2)}) async-start(), calls=%async_computation.4 | async-start | bytes 327680 | tf_op jit(solution)/shard_map/reduce_scatter | solution.py:110
  93.1 15.3 %copy-start.3 = (bf16[64,256]{1,0:T(8,128)(2,1)}, bf16[64,256]{1,0:T(8,128)(2,1)S(1)}, u32[]{:S(2)}) copy-start(bf16[64,256]{1,0:T(8,128)(2,1)S(1)} %gather_fusion) | copy-start | bytes 98308
  111.2 26.8 %copy-start.4 = (bf16[64,256]{1,0:T(8,128)(2,1)S(1)}, bf16[64,256]{1,0:T(8,128)(2,1)}, u32[]{:S(2)}) copy-start(bf16[64,256]{1,0:T(8,128)(2,1)} %copy-done.3) | copy-start | bytes 98308
Sparse Core Ops, SparseCore 0:
  117.5 20.4 reduce-scatter.1
